TPU v7x, 512 devices: a whole 4x8x8 slice. The times are simulated.
512 devices in a mesh: aux: 8 (over z), ao: 16 (over y, core), orb: 4 (over x).
Axes of the slice: x: 4, y: 8, z: 8, core: 2. Of those that a mesh axis runs over, the one named last changes fastest.
Arguments:
- integrals: bfloat16 [128, 16, 4, 128, 128], P('aux', 'ao', None, 'orb'), may hold values from -6 to 6
- partner: int32 [16, 4], P('ao'), may hold values from 0 to 15
- pair_count: int32 [16], P('ao'), may hold values from 1 to 4
- occupied_coeff: bfloat16 [2048, 512], P('ao', 'orb'), may hold values from -0.25 to 0.25
- occupied_domain: int32 [16, 4], P('ao', 'orb'), may hold values 0 or 1
- virtual_coeff: bfloat16 [2048, 8192], P('aux', 'ao'), may hold values from -0.125 to 0.125
- virtual_domain: int32 [16, 64], P(None, 'ao'), may hold values 0 or 1
Outputs:
- transformed: bfloat16 [128, 512, 8192], P('aux', 'orb', 'ao')
All inputs are finite; a program needn't handle non-finite values. No bound on the sum of `occupied_domain` or of `virtual_domain` on one device may be relied on, other than what follows from the above.
Results may differ from a plain program's by a relative error of at most 0.0049.
Values may be sent and summed in bfloat16 or wider, within the bound.
A program may use at most 64 MiB of HBM per device.

v0:
```python
import jax
import jax.numpy as jnp
from jax import lax
from jax.sharding import PartitionSpec as P


def local(
    integrals, partner, pair_count, occupied_coeff, occupied_domain, virtual_coeff, virtual_domain
):
    block_size = integrals.shape[4]
    slab_rows = integrals.shape[0]
    slot_count = integrals.shape[2]
    occ_width = occupied_coeff.shape[1]
    occ_local = occupied_coeff * occupied_domain.astype(jnp.bfloat16)
    all_occ = lax.all_gather(occ_local, "ao", axis=0, tiled=True)
    all_ints = lax.all_gather(integrals, "orb", axis=3, tiled=True)
    vir_blocks = virtual_coeff.shape[0] // block_size
    first = lax.axis_index("aux") * vir_blocks
    dom = lax.dynamic_slice_in_dim(virtual_domain, first, vir_blocks, axis=0).astype(jnp.bfloat16)
    dom = jnp.repeat(jnp.repeat(dom, block_size, axis=0), block_size, axis=1)
    vir_masked = lax.all_gather(virtual_coeff * dom, "aux", axis=0, tiled=True)
    picked = all_occ.reshape(-1, block_size, occ_width)[partner[0]]
    slots = jnp.arange(slot_count, dtype=jnp.int32)
    live = (slots < pair_count[0]).astype(jnp.bfloat16)
    picked = picked * live[:, None, None]
    half = jnp.einsum(
        "kri,pkrv->piv", picked, all_ints[:, 0], preferred_element_type=jnp.float32
    ).astype(jnp.bfloat16)
    piece = lax.all_gather(half, "ao", axis=2, tiled=True)
    flat = piece.reshape(slab_rows * occ_width, piece.shape[2])
    product = jnp.dot(flat, vir_masked, preferred_element_type=jnp.float32)
    return product.reshape(slab_rows, occ_width, -1).astype(jnp.bfloat16)


def solution(mesh):
    placed = (
        P("aux", "ao", None, "orb", None),
        P("ao", None),
        P("ao"),
        P("ao", "orb"),
        P("ao", "orb"),
        P("aux", "ao"),
        P(None, "ao"),
    )
    return jax.shard_map(
        local, mesh=mesh, in_specs=placed, out_specs=P("aux", "orb", "ao"), check_vma=False
    )
```

profile of v0, /device:TPU:1, one launch (start us, length us, event | category | flops | bytes accessed | tf_op | source)
XLA Modules:
  0.0 183.8 jit_solution(8361173918025073191)
XLA Ops:
  6.5 0.0 all-gather.4.cloned.1.call-start
  6.5 0.7 all-gather.4.cloned.1.call-update
  7.3 0.0 all-gather.8.cloned.1.call-start
  7.3 0.8 dynamic-slice_convert_fusion
  8.1 0.1 copy.8
  8.2 0.3 broadcast_in_dim.9
  8.5 1.7 bitcast_multiply_fusion
  10.2 0.0 all-gather.8.cloned.1.call-update
  10.3 0.0 all-gather.6.cloned.1.call-start
  11.6 0.7 fusion.19
  12.3 0.8 broadcast_multiply_fusion
  13.0 22.4 %all_gather.12 = bf16[2048,128]{1,0:T(8,128)(2,1)S(1)} all-gather(bf16[128,128]{1,0:T(8,128)(2,1)S(1)} %broadcast_multiply_fusion), channel_id=1, replica_groups=mesh['aux'=8,'ao'=16,'orb'=4] {'ao'}, dimensions={0}, use_global_device_ids=true | all-gather | bytes 557056 | tf_op jit(solution)/shard_map/all_gather | solution.py:15
  35.4 0.6 gather_fusion
  36.0 14.8 %all-gather.4.cloned.1.call-done = bf16[16,1,4,128,128]{4,3,2,1,0:T(8,128)(2,1)} async-done(((bf16[16,1,4,32,128]{4,3,2,1,0:T(8,128)(2,1)}), bf16[16,1,4,128,128]{4,3,2,1,0:T(8,128)(2,1)}) %all-gather.4.cloned.1.call-update) | async-done | bytes 2097168 | tf_op jit(solution)/shard_map/all_gather | solution.py:16
  50.9 2.9 %fusion.13 = bf16[16,128,128]{2,1,0:T(8,128)(2,1)} fusion(bf16[16,1,4,128,128]{4,3,2,1,0:T(8,128)(2,1)} %all-gather.4.cloned.1.call-done, bf16[4,128,128]{2,1,0:T(8,128)(2,1)S(1)} %gather_fusion, bf16[4]{0:T(256)(128)(2,1)S(1)} %compare_convert_fusion), kind=kOutput, calls=%fused_computation.8 | convolution fusion | flops 268959744 | bytes 2752520 | tf_op jit(solution)/shard_map/kri,pkrv->piv/dot_general | solution.py:26
  53.8 0.0 all-gather.6.cloned.1.call-update
  53.8 39.3 %all-gather.8.cloned.1.call-done = bf16[2048,512]{1,0:T(8,128)(2,1)} async-done(((bf16[256,512]{1,0:T(8,128)(2,1)}), bf16[2048,512]{1,0:T(8,128)(2,1)}) %all-gather.8.cloned.1.call-update) | async-done | bytes 2097168 | tf_op jit(solution)/shard_map/all_gather | solution.py:21
  93.1 74.3 %all-gather.6.cloned.1.call-done = bf16[16,128,2048]{2,1,0:T(8,128)(2,1)} async-done(((bf16[16,128,128]{2,1,0:T(8,128)(2,1)}), bf16[16,128,2048]{2,1,0:T(8,128)(2,1)}) %all-gather.6.cloned.1.call-update) | async-done | bytes 8388624 | tf_op jit(solution)/shard_map/all_gather | solution.py:29
  167.4 9.8 %fusion.4 = bf16[16,128,512]{2,1,0:T(8,128)(2,1)} fusion(bf16[16,128,2048]{2,1,0:T(8,128)(2,1)} %all-gather.6.cloned.1.call-done, bf16[2048,512]{1,0:T(8,128)(2,1)} %all-gather.8.cloned.1.call-done), kind=kOutput, calls=%fused_computation.5 | convolution fusion | flops 4296015872 | bytes 12582912 | tf_op jit(solution)/shard_map/dot_general | solution.py:31
  (3 shorter events, 0.0 us)
Async XLA Ops:
  6.5 44.3 %all-gather.4.cloned.1.call-start = ((), (), s32[]{:S(2)}) async-start(), calls=%async_computation | async-start | bytes 2621440 | tf_op jit(solution)/shard_map/all_gather | solution.py:16
  7.3 85.9 %all-gather.8.cloned.1.call-start = ((), (), s32[]{:S(2)}) async-start(), calls=%async_computation.2 | async-start | bytes 2359296 | tf_op jit(solution)/shard_map/all_gather | solution.py:21
  10.3 157.2 %all-gather.6.cloned.1.call-start = ((), (), s32[]{:S(2)}) async-start(), calls=%async_computation.1 | async-start | bytes 8912896 | tf_op jit(solution)/shard_map/all_gather | solution.py:29
Sparse Core Ops, SparseCore 0:
  9.4 41.3 all-gather.3
  52.9 40.1 all-gather.7
  95.2 72.2 all-gather.5
where the time goes:
time: 184 us
  waiting for transfers between devices  129 us (70%)
  blocking collectives  22.4 us (12%)
  between operations  14.4 us (8%)
  matrix products  12.7 us (7%)
  other arithmetic  3.9 us (2%)
    all_gather x1, waiting for transfers between devices, local(): piece = lax.all_gather(half, 'ao', axis=2, tiled=True)  74.3 us
    all_gather x1, waiting for transfers between devices, local(): vir_masked = lax.all_gather(virtual_coeff * dom, 'aux', axis=0, tiled=True)  39.3 us
    all_gather x1, blocking collectives, local(): all_occ = lax.all_gather(occ_local, 'ao', axis=0, tiled=True)  22.4 us
    all_gather x1, waiting for transfers between devices, local(): all_ints = lax.all_gather(integrals, 'orb', axis=3, tiled=True)  14.8 us
    dot_general x1, matrix products, local(): product = jnp.dot(flat, vir_masked, preferred_element_type=jnp.float32)  9.82 us
  transfers between devices with their start and end apart: 3, of which 3 were waited for; matrix products, arithmetic and copies ran while one was open for 4% of the time, Pallas kernels for 0%

commit v1 on v0

--- a/solution.py
+++ b/solution.py
@@ -18,7 +18,17 @@
     first = lax.axis_index("aux") * vir_blocks
     dom = lax.dynamic_slice_in_dim(virtual_domain, first, vir_blocks, axis=0).astype(jnp.bfloat16)
     dom = jnp.repeat(jnp.repeat(dom, block_size, axis=0), block_size, axis=1)
-    vir_masked = lax.all_gather(virtual_coeff * dom, "aux", axis=0, tiled=True)
+    x = virtual_coeff * dom
+    ways = lax.axis_size("aux")
+    up = [(d, (d + 1) % ways) for d in range(ways)]
+    down = [(d, (d - 1) % ways) for d in range(ways)]
+    earlier, later = ([x], [x])
+    for _ in range(ways // 2):
+        earlier.append(lax.ppermute(earlier[-1], "aux", up))
+    for _ in range((ways - 1) // 2):
+        later.append(lax.ppermute(later[-1], "aux", down))
+    line = jnp.concatenate([*earlier[::-1], *later[1:]], axis=0)
+    vir_masked = jnp.roll(line, (lax.axis_index("aux") - ways // 2) * x.shape[0], axis=0)
     picked = all_occ.reshape(-1, block_size, occ_width)[partner[0]]
     slots = jnp.arange(slot_count, dtype=jnp.int32)
     live = (slots < pair_count[0]).astype(jnp.bfloat16)

time: 184 us -> 141 us (0.77)
  waiting for transfers between devices: 129 us -> 53.8 us
  starting transfers between devices: 0.08 us -> 22.8 us
  local copies, waits for them, and re-layouts: 1.02 us -> 12.7 us
  other arithmetic: 3.9 us -> 1.56 us
    all_gather x1, waiting for transfers between devices: 74.3 us -> 19.5 us  [local(): piece = lax.all_gather(half, 'ao', axis=2, tiled=True)]
    all_gather x1 -> x0, waiting for transfers between devices: 39.3 us -> none  [local(): vir_masked = lax.all_gather(virtual_coeff * dom, 'aux', axis=0, tiled=True)]
    ppermute x0 -> x7, starting transfers between devices: none -> 22.7 us  [the longest x3 13.7 us: local(): later.append(lax.ppermute(later[-1], 'aux', down))]
    ppermute x0 -> x7, waiting for transfers between devices: none -> 15.6 us  [the longest x4 15.6 us: local(): earlier.append(lax.ppermute(earlier[-1], 'aux', up))]
    unnamed x0 -> x19, local copies, waits for them, and re-layouts: none -> 11 us
    all_gather x1, waiting for transfers between devices: 14.8 us -> 17.9 us  [local(): all_ints = lax.all_gather(integrals, 'orb', axis=3, tiled=True)]
  transfers between devices with their start and end apart: 3 -> 9, of which waited for: 3 -> 6; matrix products, arithmetic and copies ran while one was open for 4% -> 10% of each run, Pallas kernels for 0% -> 0%
where the time goes in v1:
time: 141 us
  waiting for transfers between devices  53.8 us (38%)
  starting transfers between devices  22.8 us (16%)
  blocking collectives  22.4 us (16%)
  between operations  14.9 us (11%)
  matrix products  12.8 us (9%)
  local copies, waits for them, and re-layouts  12.7 us (9%)
  other arithmetic  1.56 us (1%)
    all_gather x1, blocking collectives, local(): all_occ = lax.all_gather(occ_local, 'ao', axis=0, tiled=True)  22.4 us
    all_gather x1, waiting for transfers between devices, local(): piece = lax.all_gather(half, 'ao', axis=2, tiled=True)  19.5 us
    all_gather x1, waiting for transfers between devices, local(): all_ints = lax.all_gather(integrals, 'orb', axis=3, tiled=True)  17.9 us
    ppermute x4, waiting for transfers between devices, local(): earlier.append(lax.ppermute(earlier[-1], 'aux', up))  15.6 us
    ppermute x3, starting transfers between devices, local(): later.append(lax.ppermute(later[-1], 'aux', down))  13.7 us
    unnamed x19, local copies, waits for them, and re-layouts  11 us
    dot_general x1, matrix products, local(): product = jnp.dot(flat, vir_masked, preferred_element_type=jnp.float32)  9.82 us
    ppermute x4, starting transfers between devices, local(): earlier.append(lax.ppermute(earlier[-1], 'aux', up))  9 us
  transfers between devices with their start and end apart: 9, of which 6 were waited for; matrix products, arithmetic and copies ran while one was open for 10% of the time, Pallas kernels for 0%

profile of v1, /device:TPU:1, one launch (start us, length us, event | category | flops | bytes accessed | tf_op | source)
XLA Modules:
  0.0 140.8 jit_solution(7916766153099443837)
XLA Ops:
  6.5 0.0 copy-start.1
  6.5 0.0 all-gather.3.cloned.1.call-start
  6.5 0.7 all-gather.3.cloned.1.call-update
  7.3 0.0 all-gather.5.cloned.1.call-start
  8.6 0.7 fusion.20
  9.3 0.8 broadcast_multiply_fusion
  10.0 22.4 %all_gather.9 = bf16[2048,128]{1,0:T(8,128)(2,1)S(1)} all-gather(bf16[128,128]{1,0:T(8,128)(2,1)S(1)} %broadcast_multiply_fusion), channel_id=1, replica_groups=mesh['aux'=8,'ao'=16,'orb'=4] {'ao'}, dimensions={0}, use_global_device_ids=true | all-gather | bytes 557056 | tf_op jit(solution)/shard_map/all_gather | solution.py:15
  32.4 0.6 gather_fusion
  33.0 17.9 %all-gather.3.cloned.1.call-done = bf16[16,1,4,128,128]{4,3,2,1,0:T(8,128)(2,1)} async-done(((bf16[16,1,4,32,128]{4,3,2,1,0:T(8,128)(2,1)}), bf16[16,1,4,128,128]{4,3,2,1,0:T(8,128)(2,1)}) %all-gather.3.cloned.1.call-update) | async-done | bytes 2097168 | tf_op jit(solution)/shard_map/all_gather | solution.py:16
  50.9 2.9 %fusion.14 = bf16[16,128,128]{2,1,0:T(8,128)(2,1)} fusion(bf16[16,1,4,128,128]{4,3,2,1,0:T(8,128)(2,1)} %all-gather.3.cloned.1.call-done, bf16[4,128,128]{2,1,0:T(8,128)(2,1)S(1)} %gather_fusion, bf16[4]{0:T(256)(128)(2,1)S(1)} %compare_convert_fusion), kind=kOutput, calls=%fused_computation.9 | convolution fusion | flops 268959744 | bytes 2752520 | tf_op jit(solution)/shard_map/kri,pkrv->piv/dot_general | solution.py:36
  53.8 0.0 all-gather.5.cloned.1.call-update
  53.8 0.0 copy-done.1
  53.8 0.1 dynamic-slice_convert_fusion
  53.9 0.1 copy.8
  54.0 0.3 broadcast_in_dim.9
  54.4 0.0 copy-done
  54.4 3.3 %collective-permute-start = (bf16[256,512]{1,0:T(8,128)(2,1)S(1)}, bf16[256,512]{1,0:T(8,128)(2,1)S(1)}, u32[]{:S(2)}, u32[]{:S(2)}) collective-permute-start(bf16[256,512]{1,0:T(8,128)(2,1)S(1)} %bitcast_multiply_fusion), channel_id=1, source_target_pairs={{0,64},{64,128},{128,192},{192,256},{256,320},{320,384},{384,448},... | collective-permute-start | bytes 786440 | tf_op jit(solution)/shard_map/ppermute | solution.py:27
  57.7 8.1 %collective-permute-done = bf16[256,512]{1,0:T(8,128)(2,1)S(1)} collective-permute-done((bf16[256,512]{1,0:T(8,128)(2,1)S(1)}, bf16[256,512]{1,0:T(8,128)(2,1)S(1)}, u32[]{:S(2)}, u32[]{:S(2)}) %collective-permute-start) | collective-permute-done | bytes 262176 | tf_op jit(solution)/shard_map/ppermute | solution.py:27
  65.9 1.9 %collective-permute-start.1 = (bf16[256,512]{1,0:T(8,128)(2,1)S(1)}, bf16[256,512]{1,0:T(8,128)(2,1)S(1)}, u32[]{:S(2)}, u32[]{:S(2)}) collective-permute-start(bf16[256,512]{1,0:T(8,128)(2,1)S(1)} %collective-permute-done), channel_id=1, source_target_pairs={{0,64},{64,128},{128,192},{192,256},{256,320},{320,384},{384,448},... | collective-permute-start | bytes 786440 | tf_op jit(solution)/shard_map/ppermute | solution.py:27
  67.8 4.6 %collective-permute-start.4 = (bf16[256,512]{1,0:T(8,128)(2,1)S(1)}, bf16[256,512]{1,0:T(8,128)(2,1)S(1)}, u32[]{:S(2)}, u32[]{:S(2)}) collective-permute-start(bf16[256,512]{1,0:T(8,128)(2,1)S(1)} %bitcast_multiply_fusion), channel_id=1, source_target_pairs={{0,448},{64,0},{128,64},{192,128},{256,192},{320,256},{384,320},{4... | collective-permute-start | bytes 786440 | tf_op jit(solution)/shard_map/ppermute | solution.py:29
  72.4 3.2 %collective-permute-done.1 = bf16[256,512]{1,0:T(8,128)(2,1)S(1)} collective-permute-done((bf16[256,512]{1,0:T(8,128)(2,1)S(1)}, bf16[256,512]{1,0:T(8,128)(2,1)S(1)}, u32[]{:S(2)}, u32[]{:S(2)}) %collective-permute-start.1) | collective-permute-done | bytes 262176 | tf_op jit(solution)/shard_map/ppermute | solution.py:27
  75.5 1.9 %collective-permute-start.2 = (bf16[256,512]{1,0:T(8,128)(2,1)S(1)}, bf16[256,512]{1,0:T(8,128)(2,1)S(1)}, u32[]{:S(2)}, u32[]{:S(2)}) collective-permute-start(bf16[256,512]{1,0:T(8,128)(2,1)S(1)} %collective-permute-done.1), channel_id=1, source_target_pairs={{0,64},{64,128},{128,192},{192,256},{256,320},{320,384},{384,448},... | collective-permute-start | bytes 786440 | tf_op jit(solution)/shard_map/ppermute | solution.py:27
  77.4 0.0 collective-permute-done.4
  77.4 4.6 %collective-permute-start.5 = (bf16[256,512]{1,0:T(8,128)(2,1)S(1)}, bf16[256,512]{1,0:T(8,128)(2,1)S(1)}, u32[]{:S(2)}, u32[]{:S(2)}) collective-permute-start(bf16[256,512]{1,0:T(8,128)(2,1)S(1)} %collective-permute-done.4), channel_id=1, source_target_pairs={{0,448},{64,0},{128,64},{192,128},{256,192},{320,256},{384,320},{4... | collective-permute-start | bytes 786440 | tf_op jit(solution)/shard_map/ppermute | solution.py:29
  82.0 2.4 %collective-permute-done.2 = bf16[256,512]{1,0:T(8,128)(2,1)S(1)} collective-permute-done((bf16[256,512]{1,0:T(8,128)(2,1)S(1)}, bf16[256,512]{1,0:T(8,128)(2,1)S(1)}, u32[]{:S(2)}, u32[]{:S(2)}) %collective-permute-start.2) | collective-permute-done | bytes 262176 | tf_op jit(solution)/shard_map/ppermute | solution.py:27
  84.4 1.9 %collective-permute-start.3 = (bf16[256,512]{1,0:T(8,128)(2,1)S(1)}, bf16[256,512]{1,0:T(8,128)(2,1)S(1)}, u32[]{:S(2)}, u32[]{:S(2)}) collective-permute-start(bf16[256,512]{1,0:T(8,128)(2,1)S(1)} %collective-permute-done.2), channel_id=1, source_target_pairs={{0,64},{64,128},{128,192},{192,256},{256,320},{320,384},{384,448},... | collective-permute-start | bytes 786440 | tf_op jit(solution)/shard_map/ppermute | solution.py:27
  86.4 0.0 collective-permute-done.5
  86.4 4.6 %collective-permute-start.6 = (bf16[256,512]{1,0:T(8,128)(2,1)S(1)}, bf16[256,512]{1,0:T(8,128)(2,1)S(1)}, u32[]{:S(2)}, u32[]{:S(2)}) collective-permute-start(bf16[256,512]{1,0:T(8,128)(2,1)S(1)} %collective-permute-done.5), channel_id=1, source_target_pairs={{0,448},{64,0},{128,64},{192,128},{256,192},{320,256},{384,320},{4... | collective-permute-start | bytes 786440 | tf_op jit(solution)/shard_map/ppermute | solution.py:29
  90.9 2.0 %collective-permute-done.3 = bf16[256,512]{1,0:T(8,128)(2,1)S(1)} collective-permute-done((bf16[256,512]{1,0:T(8,128)(2,1)S(1)}, bf16[256,512]{1,0:T(8,128)(2,1)S(1)}, u32[]{:S(2)}, u32[]{:S(2)}) %collective-permute-start.3) | collective-permute-done | bytes 262176 | tf_op jit(solution)/shard_map/ppermute | solution.py:27
  92.9 0.7 constant_dynamic-update-slice_fusion.15
  93.6 0.7 constant_dynamic-update-slice_fusion.14
  94.4 0.8 constant_dynamic-update-slice_fusion.13
  95.1 0.7 constant_dynamic-update-slice_fusion.12
  95.9 0.7 constant_dynamic-update-slice_fusion.11
  96.6 0.7 constant_dynamic-update-slice_fusion.10
  97.3 0.7 constant_dynamic-update-slice_fusion.9
  98.0 0.0 collective-permute-done.6
  98.0 0.7 constant_dynamic-update-slice_fusion.8
  98.8 0.7 constant_dynamic-update-slice_fusion.7
  99.5 0.7 constant_dynamic-update-slice_fusion.6
  100.2 0.7 constant_dynamic-update-slice_fusion.5
  101.0 0.7 constant_dynamic-update-slice_fusion.4
  101.7 0.7 constant_dynamic-update-slice_fusion.3
  102.4 0.7 constant_dynamic-update-slice_fusion.2
  103.1 0.7 constant_dynamic-update-slice_fusion.1
  103.9 0.7 constant_dynamic-update-slice_fusion
  104.6 19.5 %all-gather.5.cloned.1.call-done = bf16[16,128,2048]{2,1,0:T(8,128)(2,1)} async-done(((bf16[16,128,128]{2,1,0:T(8,128)(2,1)}), bf16[16,128,2048]{2,1,0:T(8,128)(2,1)}) %all-gather.5.cloned.1.call-update) | async-done | bytes 8388624 | tf_op jit(solution)/shard_map/all_gather | solution.py:39
  124.1 9.8 %fusion.5 = bf16[16,128,512]{2,1,0:T(8,128)(2,1)} fusion(bf16[16,128,2048]{2,1,0:T(8,128)(2,1)} %all-gather.5.cloned.1.call-done, bf16[4096,512]{1,0:T(8,128)(2,1)} %constant_dynamic-update-slice_fusion, s32[]{:T(128)S(6)} %select_n.29), kind=kOutput, calls=%fused_computation.6 | convolution fusion | flops 4296015872 | bytes 12582916 | tf_op jit(solution)/shard_map/dot_general | solution.py:41
  (5 shorter events, 0.1 us)
Async XLA Ops:
  6.5 47.3 %copy-start.1 = (s32[16,4]{0,1:T(4,128)S(1)}, s32[16,4]{0,1:T(4,128)}, u32[]{:S(2)}) copy-start(s32[16,4]{0,1:T(4,128)} %param.13) | copy-start | bytes 772
  6.5 47.9 %copy-start = (bf16[256,512]{1,0:T(8,128)(2,1)S(1)}, bf16[256,512]{1,0:T(8,128)(2,1)}, u32[]{:S(2)}) copy-start(bf16[256,512]{1,0:T(8,128)(2,1)} %param.12) | copy-start | bytes 786436
  6.5 44.3 %all-gather.3.cloned.1.call-start = ((), (), s32[]{:S(2)}) async-start(), calls=%async_computation | async-start | bytes 2621440 | tf_op jit(solution)/shard_map/all_gather | solution.py:16
  7.3 116.9 %all-gather.5.cloned.1.call-start = ((), (), s32[]{:S(2)}) async-start(), calls=%async_computation.1 | async-start | bytes 8912896 | tf_op jit(solution)/shard_map/all_gather | solution.py:39
  54.4 11.4 %collective-permute-start = (bf16[256,512]{1,0:T(8,128)(2,1)S(1)}, bf16[256,512]{1,0:T(8,128)(2,1)S(1)}, u32[]{:S(2)}, u32[]{:S(2)}) collective-permute-start(bf16[256,512]{1,0:T(8,128)(2,1)S(1)} %bitcast_multiply_fusion), channel_id=1, source_target_pairs={{0,64},{64,128},{128,192},{192,256},{256,320},{320,384},{384,448},... | collective-permute-start | bytes 786440 | tf_op jit(solution)/shard_map/ppermute | solution.py:27
  65.9 9.6 %collective-permute-start.1 = (bf16[256,512]{1,0:T(8,128)(2,1)S(1)}, bf16[256,512]{1,0:T(8,128)(2,1)S(1)}, u32[]{:S(2)}, u32[]{:S(2)}) collective-permute-start(bf16[256,512]{1,0:T(8,128)(2,1)S(1)} %collective-permute-done), channel_id=1, source_target_pairs={{0,64},{64,128},{128,192},{192,256},{256,320},{320,384},{384,448},... | collective-permute-start | bytes 786440 | tf_op jit(solution)/shard_map/ppermute | solution.py:27
  67.8 9.7 %collective-permute-start.4 = (bf16[256,512]{1,0:T(8,128)(2,1)S(1)}, bf16[256,512]{1,0:T(8,128)(2,1)S(1)}, u32[]{:S(2)}, u32[]{:S(2)}) collective-permute-start(bf16[256,512]{1,0:T(8,128)(2,1)S(1)} %bitcast_multiply_fusion), channel_id=1, source_target_pairs={{0,448},{64,0},{128,64},{192,128},{256,192},{320,256},{384,320},{4... | collective-permute-start | bytes 786440 | tf_op jit(solution)/shard_map/ppermute | solution.py:29
  75.5 8.9 %collective-permute-start.2 = (bf16[256,512]{1,0:T(8,128)(2,1)S(1)}, bf16[256,512]{1,0:T(8,128)(2,1)S(1)}, u32[]{:S(2)}, u32[]{:S(2)}) collective-permute-start(bf16[256,512]{1,0:T(8,128)(2,1)S(1)} %collective-permute-done.1), channel_id=1, source_target_pairs={{0,64},{64,128},{128,192},{192,256},{256,320},{320,384},{384,448},... | collective-permute-start | bytes 786440 | tf_op jit(solution)/shard_map/ppermute | solution.py:27
  77.4 8.9 %collective-permute-start.5 = (bf16[256,512]{1,0:T(8,128)(2,1)S(1)}, bf16[256,512]{1,0:T(8,128)(2,1)S(1)}, u32[]{:S(2)}, u32[]{:S(2)}) collective-permute-start(bf16[256,512]{1,0:T(8,128)(2,1)S(1)} %collective-permute-done.4), channel_id=1, source_target_pairs={{0,448},{64,0},{128,64},{192,128},{256,192},{320,256},{384,320},{4... | collective-permute-start | bytes 786440 | tf_op jit(solution)/shard_map/ppermute | solution.py:29
  84.4 8.5 %collective-permute-start.3 = (bf16[256,512]{1,0:T(8,128)(2,1)S(1)}, bf16[256,512]{1,0:T(8,128)(2,1)S(1)}, u32[]{:S(2)}, u32[]{:S(2)}) collective-permute-start(bf16[256,512]{1,0:T(8,128)(2,1)S(1)} %collective-permute-done.2), channel_id=1, source_target_pairs={{0,64},{64,128},{128,192},{192,256},{256,320},{320,384},{384,448},... | collective-permute-start | bytes 786440 | tf_op jit(solution)/shard_map/ppermute | solution.py:27
  86.4 11.7 %collective-permute-start.6 = (bf16[256,512]{1,0:T(8,128)(2,1)S(1)}, bf16[256,512]{1,0:T(8,128)(2,1)S(1)}, u32[]{:S(2)}, u32[]{:S(2)}) collective-permute-start(bf16[256,512]{1,0:T(8,128)(2,1)S(1)} %collective-permute-done.5), channel_id=1, source_target_pairs={{0,448},{64,0},{128,64},{192,128},{256,192},{320,256},{384,320},{4... | collective-permute-start | bytes 786440 | tf_op jit(solution)/shard_map/ppermute | solution.py:29
Sparse Core Ops, SparseCore 0:
  9.4 41.3 all-gather.2
  54.0 70.1 all-gather.4
